TPU v7x, 32 devices: a whole 2x2x4 slice. The times are simulated.
32 devices in a mesh: groups: 2 (over y), rows: 4 (over z), blocks: 2 (over x), cols: 2 (over core).
Axes of the slice: x: 2, y: 2, z: 4, core: 2. Of those that a mesh axis runs over, the one named last changes fastest.
Arguments:
- inputs: bfloat16 [4096, 1024], P(('groups', 'rows')), parts along dimension 0, may hold values from -6 to 6
- projection: bfloat16 [1024, 8192], P(None, ('groups', 'blocks', 'cols')), parts along dimension 1, may hold values from -0.1875 to 0.1875
- phases: bfloat16 [8192], P(('groups', 'blocks', 'cols')), parts along dimension 0, may hold values from -3.140625 to 3.140625
- inverse_blocks: float32 [4, 2048, 2048], P(('groups', 'blocks'), 'rows'), parts along dimension 0, as said below
- labels: int32 [4096], P(('groups', 'rows')), parts along dimension 0, may hold values from 0 to 999
- predictions: float32 [4096, 1000], P(('groups', 'rows'), 'cols'), parts along dimension 0, may hold values from -4 to 4
- coefficients: float32 [8192, 1000], P(('groups', 'blocks', 'rows'), 'cols'), parts along dimension 0, may hold values from -3 to 3
Outputs:
- new_coefficients: float32 [8192, 1000], P(('groups', 'blocks', 'rows'), 'cols'), parts along dimension 0
- new_predictions: float32 [4096, 1000], P(('groups', 'rows'), 'cols'), parts along dimension 0
There are 2 independent parts, one for each index of `groups`. A program takes and returns all parts, laid end to end along the dimension named above; each array names one. Nothing has to cross between parts.
Inputs may be any that keep to these rules, and one draw needn't show every extreme that they name: `inverse_blocks`: one dense preconditioner for each feature block.
All inputs are finite; a program needn't handle non-finite values.
Results may differ from a plain program's by a relative error of at most 0.0029.
Values may be sent and summed in bfloat16 or wider, within the bound.
No kernel may reach another device: no remote copies, remote signals or barrier semaphores. Data moves between devices by JAX's collectives and lax.ppermute only.
A program may use at most 64 MiB of HBM per device.

v0:
```python
import jax
import jax.numpy as jnp
from jax import lax
from jax.sharding import PartitionSpec as P

DAMPING = 0.5


def cosine_features(inputs, projection, phases):
    angles = (
        jnp.dot(inputs, projection, preferred_element_type=jnp.float32)
        + phases.astype(jnp.float32)[None, :]
    )
    return jnp.cos(angles).astype(jnp.bfloat16)


def shards(inputs, projection, phases, inverse_blocks, labels, predictions, coefficients):
    out_width = predictions.shape[1]
    classes = lax.axis_index("cols") * out_width + jnp.arange(out_width, dtype=jnp.int32)
    onehot = (labels[:, None] == classes[None, :]).astype(jnp.float32)
    residual = (onehot - predictions).astype(jnp.bfloat16)
    half_features = cosine_features(inputs, projection, phases)
    features_full = lax.all_gather(half_features, "cols", axis=1, tiled=True)
    local_inverse = inverse_blocks[0]
    column_slice = features_full
    own_gradient = lax.psum_scatter(
        lax.dot_general(
            column_slice, residual, (((0,), (0,)), ((), ())), preferred_element_type=jnp.float32
        ),
        "rows",
        scatter_dimension=0,
        tiled=True,
    )
    gradient = lax.all_gather(own_gradient, "rows", axis=0, tiled=True)
    solved = jnp.dot(local_inverse, gradient, precision=lax.Precision.HIGHEST)
    step_update = DAMPING * solved
    new_coefficients = coefficients + step_update
    column_slice = features_full
    contribution = jnp.dot(
        column_slice,
        lax.all_gather(step_update.astype(jnp.bfloat16), "rows", axis=0, tiled=True),
        preferred_element_type=jnp.float32,
    )
    summed = lax.psum(contribution, "blocks")
    return (new_coefficients, predictions + summed)


def solution(mesh):
    return jax.shard_map(
        shards,
        mesh=mesh,
        in_specs=(
            P(("groups", "rows"), None),
            P(None, ("groups", "blocks", "cols")),
            P(("groups", "blocks", "cols")),
            P(("groups", "blocks"), "rows", None),
            P(("groups", "rows")),
            P(("groups", "rows"), "cols"),
            P(("groups", "blocks", "rows"), "cols"),
        ),
        out_specs=(P(("groups", "blocks", "rows"), "cols"), P(("groups", "rows"), "cols")),
        check_vma=False,
    )
```

profile of v0, /device:TPU:0, one launch (start us, length us, event | category | flops | bytes accessed | tf_op | source)
XLA Modules:
  0.0 311.2 jit_solution(1773116370345842166)
XLA Ops:
  7.2 0.0 copy-start
  7.2 0.0 all-gather.4.cloned.1.call-start
  7.2 0.8 convert_element_type.15
  8.0 0.7 copy-done
  8.8 0.0 copy-start.1
  8.8 0.0 copy-start.2
  8.8 9.8 %cosine_convert_fusion = bf16[512,1024]{1,0:T(8,128)(2,1)} fusion(bf16[512,1024]{1,0:T(8,128)(2,1)} %param.7, bf16[1024,1024]{1,0:T(8,128)(2,1)S(1)} %copy-done, f32[1024]{0:T(1024)S(1)} %convert_element_type.15), kind=kOutput, calls=%fused_computation.2 | convolution fusion | flops 1074790400 | bytes 4198400 | tf_op jit(solution)/shard_map/dot_general | solution.py:11
  18.6 0.0 all-gather.4.cloned.1.call-update
  18.6 0.0 reduce-scatter.2.cloned.1.call-start
  18.7 13.4 %all-gather.4.cloned.1.call-done = bf16[512,2048]{1,0:T(8,128)(2,1)} async-done(((bf16[512,1024]{1,0:T(8,128)(2,1)}), bf16[512,2048]{1,0:T(8,128)(2,1)}) %all-gather.4.cloned.1.call-update) | async-done | bytes 2097168 | tf_op jit(solution)/shard_map/all_gather | solution.py:23
  32.1 0.0 copy-done.1
  32.1 0.0 copy-done.2
  32.1 5.0 %fusion.8 = f32[2048,500]{1,0:T(8,128)} fusion(bf16[512,2048]{1,0:T(8,128)(2,1)} %all-gather.4.cloned.1.call-done, f32[512,500]{0,1:T(8,128)S(1)} %copy-done.1, s32[512]{0:T(512)S(1)} %copy-done.2, s32[500]{0:T(512)S(1)} %iota_add_fusion), kind=kOutput, calls=%fused_computation.6 | convolution fusion | flops 1049600000 | bytes 7221200 | tf_op jit(solution)/shard_map/dot_general | solution.py:27
  37.0 0.0 reduce-scatter.2.cloned.1.call-update
  37.0 0.0 all-gather.6.cloned.1.call-start
  37.1 78.0 %reduce-scatter.2.cloned.1.call-done = f32[512,500]{1,0:T(8,128)} async-done(((f32[2048,500]{1,0:T(8,128)}), f32[512,500]{1,0:T(8,128)}) %reduce-scatter.2.cloned.1.call-update) | async-done | bytes 1024016 | tf_op jit(solution)/shard_map/reduce_scatter | solution.py:26
  115.1 0.0 all-gather.6.cloned.1.call-update
  115.2 0.2 all-gather.8.cloned.1.call-start
  115.4 82.7 %all-gather.6.cloned.1.call-done = f32[2048,500]{1,0:T(8,128)} async-done(((f32[512,500]{1,0:T(8,128)}), f32[2048,500]{1,0:T(8,128)}) %all-gather.6.cloned.1.call-update) | async-done | bytes 4096016 | tf_op jit(solution)/shard_map/all_gather | solution.py:34
  198.1 17.2 %fusion.11 = (bf16[512,500]{0,1:T(8,128)(2,1)}, f32[512,500]{0,1:T(8,128)}) fusion(f32[512,500]{0,1:T(8,128)} %param.13, f32[2048,500]{1,0:T(8,128)} %all-gather.6.cloned.1.call-done, f32[1,512,2048]{2,1,0:T(8,128)} %param.10), kind=kOutput, calls=%fused_computation.10 | convolution fusion | flops 6292224000 | bytes 10850304 | tf_op jit(solution)/shard_map/dot_general | solution.py:35
  215.3 0.0 all-gather.8.cloned.1.call-update
  215.3 0.0 all-reduce.2.cloned.1.call-start
  215.4 43.9 %all-gather.8.cloned.1.call-done = bf16[2048,500]{0,1:T(8,128)(2,1)} async-done(((bf16[512,500]{0,1:T(8,128)(2,1)}), bf16[2048,500]{0,1:T(8,128)(2,1)}) %all-gather.8.cloned.1.call-update) | async-done | bytes 2048016 | tf_op jit(solution)/shard_map/all_gather | solution.py:41
  259.3 4.4 %fusion.12 = f32[512,500]{0,1:T(8,128)} fusion(bf16[512,2048]{1,0:T(8,128)(2,1)} %all-gather.4.cloned.1.call-done, bf16[2048,500]{0,1:T(8,128)(2,1)} %all-gather.8.cloned.1.call-done), kind=kOutput, calls=%fused_computation.11 | convolution fusion | flops 1048576000 | bytes 5169152 | tf_op jit(solution)/shard_map/dot_general | solution.py:39
  263.7 0.0 all-reduce.2.cloned.1.call-update
  263.8 38.6 %all-reduce.2.cloned.1.call-done = f32[512,500]{0,1:T(8,128)} async-done(((f32[512,500]{0,1:T(8,128)}), f32[512,500]{0,1:T(8,128)}) %all-reduce.2.cloned.1.call-update) | async-done | bytes 1024016 | tf_op jit(solution)/shard_map/psum | solution.py:44
  302.3 2.4 add.33
  (1 shorter events, 0.0 us)
Async XLA Ops:
  7.2 1.6 copy-start
  7.2 24.9 %all-gather.4.cloned.1.call-start = ((), (), s32[]{:S(2)}) async-start(), calls=%async_computation.1 | async-start | bytes 3145728 | tf_op jit(solution)/shard_map/all_gather | solution.py:23
  8.8 23.3 %copy-start.1 = (f32[512,500]{0,1:T(8,128)S(1)}, f32[512,500]{0,1:T(8,128)}, u32[]{:S(2)}) copy-start(f32[512,500]{0,1:T(8,128)} %param.12) | copy-start | bytes 3072004
  8.8 23.3 %copy-start.2 = (s32[512]{0:T(512)S(1)}, s32[512]{0:T(512)}, u32[]{:S(2)}) copy-start(s32[512]{0:T(512)} %param.11) | copy-start | bytes 6148
  18.6 96.5 %reduce-scatter.2.cloned.1.call-start = ((), (), s32[]{:S(2)}) async-start(), calls=%async_computation.2 | async-start | bytes 5242880 | tf_op jit(solution)/shard_map/reduce_scatter | solution.py:26
  37.0 161.1 %all-gather.6.cloned.1.call-start = ((), (), s32[]{:S(2)}) async-start(), calls=%async_computation.3 | async-start | bytes 5242880 | tf_op jit(solution)/shard_map/all_gather | solution.py:34
  115.2 144.1 %all-gather.8.cloned.1.call-start = ((), (), s32[]{:S(2)}) async-start(), calls=%async_computation.4 | async-start | bytes 2580480 | tf_op jit(solution)/shard_map/all_gather | solution.py:41
  215.3 87.0 %all-reduce.2.cloned.1.call-start = ((), (), s32[]{:S(2)}) async-start(), calls=%async_computation.5 | async-start | bytes 2064384 | tf_op jit(solution)/shard_map/psum | solution.py:44
Sparse Core Ops, SparseCore 0:
  18.7 13.2 all-gather.3
  37.2 77.9 reduce-scatter.1
  116.8 81.2 all-gather.5
  215.4 43.8 all-gather.7
  263.9 38.3 all-reduce.1
where the time goes:
time: 311 us
  waiting for transfers between devices  257 us (83%)
  matrix products  36.4 us (12%)
  between operations  13.8 us (4%)
  other arithmetic  3.21 us (1%)
    all_gather x1, waiting for transfers between devices, shards(): gradient = lax.all_gather(own_gradient, 'rows', axis=0, tiled=True)  82.7 us
    reduce_scatter x1, waiting for transfers between devices, shards(): lax.psum_scatter(lax.dot_general(column_slice, residual, (((0,), (0,)), (...  78 us
    all_gather x1, waiting for transfers between devices, shards(): lax.all_gather(step_update.astype(jnp.bfloat16), 'rows', axis=0, tiled=True)  43.9 us
    psum x1, waiting for transfers between devices, shards(): summed = lax.psum(contribution, 'blocks')  38.6 us
    dot_general x1, matrix products, shards(): solved = jnp.dot(local_inverse, gradient, precision=lax.Precision.HIGHEST)  17.2 us
    all_gather x1, waiting for transfers between devices, shards(): features_full = lax.all_gather(half_features, 'cols', axis=1, tiled=True)  13.4 us
    dot_general x1, matrix products, cosine_features(): jnp.dot(inputs, projection, preferred_element_type=jnp.float32)  9.81 us
  transfers between devices with their start and end apart: 5, of which 5 were waited for; matrix products, arithmetic and copies ran while one was open for 0% of the time, Pallas kernels for 0%

commit v1 on v0

--- a/solution.py
+++ b/solution.py
@@ -1,9 +1,41 @@
+import functools
 import jax
 import jax.numpy as jnp
 from jax import lax
 from jax.sharding import PartitionSpec as P
 
 DAMPING = 0.5
+
+
+def replace_the_lines(mine_x, d0):
+    mine_x = jnp.moveaxis(mine_x, 0, d0)
+    before = mine_x.shape
+    after = mine_x.reshape(*before[:d0], before[d0] * before[d0 + 1], *before[d0 + 2 :])
+    return after
+
+
+def _search_bars(my_data, comm_axis):
+    z = lax.axis_index(comm_axis)
+    b_next = lax.axis_size(comm_axis)
+    tmp, g_now = (b_next, z)
+    tall, main = (my_data[None], 1)
+    while main < tmp:
+        block_now = lax.ppermute(tall, comm_axis, perm=[(h, h ^ main) for h in range(tmp)])
+        right_arr = g_now & main == 0
+        tall = jnp.concatenate(
+            [jnp.where(right_arr, tall, block_now), jnp.where(right_arr, block_now, tall)]
+        )
+        main *= 2
+    return tall
+
+
+def _keep_up_cube(local_block, xx, dimension_no):
+    next_value = _search_bars(local_block, xx)
+    spare = replace_the_lines(next_value, dimension_no)
+    return spare
+
+
+teams_compute = functools.partial(_keep_up_cube, xx="rows", dimension_no=0)
 
 
 def cosine_features(inputs, projection, phases):
@@ -38,7 +70,7 @@
     column_slice = features_full
     contribution = jnp.dot(
         column_slice,
-        lax.all_gather(step_update.astype(jnp.bfloat16), "rows", axis=0, tiled=True),
+        teams_compute(step_update.astype(jnp.bfloat16)),
         preferred_element_type=jnp.float32,
     )
     summed = lax.psum(contribution, "blocks")

time: 311 us -> 330 us (1.061)
  waiting for transfers between devices: 257 us -> 269 us
  local copies, waits for them, and re-layouts: 0.74 us -> 7.43 us
  matrix products: 36.4 us -> 29.8 us
  other arithmetic: 3.21 us -> 7.51 us
    ppermute x0 -> x2, waiting for transfers between devices: none -> 58.6 us  [_search_bars(): lax.ppermute(tall, comm_axis, perm=[(h, h ^ main) for h in range(tmp)])]
    all_gather x1 -> x0, waiting for transfers between devices: 43.9 us -> none  [shards(): lax.all_gather(step_update.astype(jnp.bfloat16), 'rows', axis=0, tiled=True)]
    dot_general x1, matrix products: 17.2 us -> 10.6 us  [shards(): solved = jnp.dot(local_inverse, gradient, precision=lax.Precision.HIGHEST)]
    concatenate x0 -> x2, local copies, waits for them, and re-layouts: none -> 5.91 us  [_search_bars(): jnp.concatenate([jnp.where(right_arr, tall, block_now), jnp.where(right_a...]
  transfers between devices with their start and end apart: 5 -> 6, of which waited for: 5 -> 6; matrix products, arithmetic and copies ran while one was open for 0% -> 0% of each run, Pallas kernels for 0% -> 0%
where the time goes in v1:
time: 330 us; the launch traced here: 329 us
  waiting for transfers between devices  269 us (82%)
  matrix products  29.8 us (9%)
  between operations  13.8 us (4%)
  other arithmetic  7.51 us (2%)
  local copies, waits for them, and re-layouts  7.43 us (2%)
    all_gather x1, waiting for transfers between devices, shards(): gradient = lax.all_gather(own_gradient, 'rows', axis=0, tiled=True)  81.6 us
    reduce_scatter x1, waiting for transfers between devices, shards(): lax.psum_scatter(lax.dot_general(column_slice, residual, (((0,), (0,)), (...  77 us
    ppermute x2, waiting for transfers between devices, _search_bars(): lax.ppermute(tall, comm_axis, perm=[(h, h ^ main) for h in range(tmp)])  58.6 us
    psum x1, waiting for transfers between devices, shards(): summed = lax.psum(contribution, 'blocks')  38.7 us
    all_gather x1, waiting for transfers between devices, shards(): features_full = lax.all_gather(half_features, 'cols', axis=1, tiled=True)  13.4 us
    dot_general x1, matrix products, shards(): solved = jnp.dot(local_inverse, gradient, precision=lax.Precision.HIGHEST)  10.6 us
    dot_general x1, matrix products, cosine_features(): jnp.dot(inputs, projection, preferred_element_type=jnp.float32)  9.83 us
  transfers between devices with their start and end apart: 6, of which 6 were waited for; matrix products, arithmetic and copies ran while one was open for 0% of the time, Pallas kernels for 0%

profile of v1, /device:TPU:0, one launch (start us, length us, event | category | flops | bytes accessed | tf_op | source)
XLA Modules:
  0.0 329.2 jit_solution(3186903916985230293)
XLA Ops:
  7.2 0.0 copy-start
  7.2 0.0 all-gather.3.cloned.1.call-start
  7.2 0.8 convert_element_type.15
  8.0 0.7 copy-done
  8.8 0.0 copy-start.1
  8.8 0.0 copy-start.4
  8.8 9.8 %cosine_convert_fusion = bf16[512,1024]{1,0:T(8,128)(2,1)} fusion(bf16[512,1024]{1,0:T(8,128)(2,1)} %param.7, bf16[1024,1024]{1,0:T(8,128)(2,1)S(1)} %copy-done, f32[1024]{0:T(1024)S(1)} %convert_element_type.15), kind=kOutput, calls=%fused_computation.2 | convolution fusion | flops 1074790400 | bytes 4198400 | tf_op jit(solution)/shard_map/dot_general | solution.py:43
  18.6 0.0 all-gather.3.cloned.1.call-update
  18.6 0.0 reduce-scatter.2.cloned.1.call-start
  18.7 13.4 %all-gather.3.cloned.1.call-done = bf16[512,2048]{1,0:T(8,128)(2,1)} async-done(((bf16[512,1024]{1,0:T(8,128)(2,1)}), bf16[512,2048]{1,0:T(8,128)(2,1)}) %all-gather.3.cloned.1.call-update) | async-done | bytes 2097168 | tf_op jit(solution)/shard_map/all_gather | solution.py:55
  32.1 0.0 copy-done.1
  32.1 0.0 copy-done.4
  32.1 4.8 %fusion.8 = f32[2048,500]{0,1:T(8,128)} fusion(bf16[512,2048]{1,0:T(8,128)(2,1)} %all-gather.3.cloned.1.call-done, f32[512,500]{0,1:T(8,128)S(1)} %copy-done.1, s32[512]{0:T(512)S(1)} %copy-done.4, s32[500]{0:T(512)S(1)} %iota_add_fusion), kind=kOutput, calls=%fused_computation.10 | convolution fusion | flops 1049600000 | bytes 7221200 | tf_op jit(solution)/shard_map/dot_general | solution.py:59
  36.9 0.0 reduce-scatter.2.cloned.1.call-update
  36.9 0.0 all-gather.5.cloned.1.call-start
  37.0 77.0 %reduce-scatter.2.cloned.1.call-done = f32[512,500]{0,1:T(8,128)} async-done(((f32[2048,500]{0,1:T(8,128)}), f32[512,500]{0,1:T(8,128)}) %reduce-scatter.2.cloned.1.call-update) | async-done | bytes 1024016 | tf_op jit(solution)/shard_map/reduce_scatter | solution.py:58
  114.0 0.0 all-gather.5.cloned.1.call-update
  114.0 0.2 all-reduce.2.cloned.1.call-start
  114.2 81.6 %all-gather.5.cloned.1.call-done = f32[2048,500]{0,1:T(8,128)} async-done(((f32[512,500]{0,1:T(8,128)}), f32[2048,500]{0,1:T(8,128)}) %all-gather.5.cloned.1.call-update) | async-done | bytes 4096016 | tf_op jit(solution)/shard_map/all_gather | solution.py:66
  195.8 10.6 %convert_bitcast_fusion = (bf16[1,512,500]{1,2,0:T(8,128)(2,1)S(1)}, f32[512,500]{0,1:T(8,128)}) fusion(f32[512,500]{0,1:T(8,128)} %param.13, f32[2048,500]{0,1:T(8,128)} %all-gather.5.cloned.1.call-done, f32[1,512,2048]{2,1,0:T(8,128)} %param.10), kind=kOutput, calls=%fused_computation.11 | convolution fusion | flops 6292224000 | bytes 10850304 | tf_op jit(solution)/shard_map/dot_general | solution.py:67
  206.4 0.0 copy-start.3
  206.4 0.0 collective-permute-start
  206.5 0.8 copy-done.3
  207.2 12.8 %collective-permute-done = bf16[1,512,500]{1,2,0:T(8,128)(2,1)} collective-permute-done((bf16[1,512,500]{1,2,0:T(8,128)(2,1)S(1)}, bf16[1,512,500]{1,2,0:T(8,128)(2,1)}, u32[]{:S(2)}, u32[]{:S(2)}) %collective-permute-start) | collective-permute-done | bytes 512032 | tf_op jit(solution)/shard_map/ppermute | solution.py:23
  220.1 1.3 broadcast_select_fusion.3
  221.3 0.1 pad_maximum_fusion.1
  221.4 1.7 copy.10
  223.2 0.9 collective-permute-start.1
  224.1 45.8 %collective-permute-done.1 = bf16[2,512,500]{1,0,2:T(2,128)(2,1)} collective-permute-done((bf16[2,512,500]{1,0,2:T(2,128)(2,1)}, bf16[2,512,500]{1,0,2:T(2,128)(2,1)}, u32[]{:S(2)}, u32[]{:S(2)}) %collective-permute-start.1) | collective-permute-done | bytes 1024032 | tf_op jit(solution)/shard_map/ppermute | solution.py:23
  269.8 1.4 broadcast_select_fusion.1
  271.3 1.5 pad_maximum_fusion
  272.8 4.2 %copy.13 = bf16[4,512,500]{2,1,0:T(8,128)(2,1)} copy(bf16[4,512,500]{1,2,0:T(8,128)(2,1)} %pad_maximum_fusion) | data formatting | bytes 4096000 | tf_op jit(solution)/shard_map/concatenate | solution.py:25
  277.0 0.0 copy-start.2
  277.0 4.5 %fusion.13 = f32[512,500]{0,1:T(8,128)} fusion(bf16[512,2048]{1,0:T(8,128)(2,1)} %all-gather.3.cloned.1.call-done, bf16[2048,500]{1,0:T(8,128)(2,1)} %bitcast.22), kind=kOutput, calls=%fused_computation.17 | convolution fusion | flops 1048576000 | bytes 5169152 | tf_op jit(solution)/shard_map/dot_general | solution.py:71
  281.5 0.0 all-reduce.2.cloned.1.call-update
  281.5 38.7 %all-reduce.2.cloned.1.call-done = f32[512,500]{0,1:T(8,128)} async-done(((f32[512,500]{0,1:T(8,128)}), f32[512,500]{0,1:T(8,128)}) %all-reduce.2.cloned.1.call-update) | async-done | bytes 1024016 | tf_op jit(solution)/shard_map/psum | solution.py:76
  320.2 0.0 copy-done.2
  320.3 2.4 add.33
  (1 shorter events, 0.0 us)
Async XLA Ops:
  7.2 1.6 copy-start
  7.2 24.9 %all-gather.3.cloned.1.call-start = ((), (), s32[]{:S(2)}) async-start(), calls=%async_computation.1 | async-start | bytes 3145728 | tf_op jit(solution)/shard_map/all_gather | solution.py:55
  8.8 23.3 %copy-start.1 = (f32[512,500]{0,1:T(8,128)S(1)}, f32[512,500]{0,1:T(8,128)}, u32[]{:S(2)}) copy-start(f32[512,500]{0,1:T(8,128)} %param.12) | copy-start | bytes 3072004
  8.8 23.3 %copy-start.4 = (s32[512]{0:T(512)S(1)}, s32[512]{0:T(512)}, u32[]{:S(2)}) copy-start(s32[512]{0:T(512)} %param.11) | copy-start | bytes 6148
  18.6 95.4 %reduce-scatter.2.cloned.1.call-start = ((), (), s32[]{:S(2)}) async-start(), calls=%async_computation.2 | async-start | bytes 5160960 | tf_op jit(solution)/shard_map/reduce_scatter | solution.py:58
  36.9 158.9 %all-gather.5.cloned.1.call-start = ((), (), s32[]{:S(2)}) async-start(), calls=%async_computation.3 | async-start | bytes 5160960 | tf_op jit(solution)/shard_map/all_gather | solution.py:66
  114.0 206.2 %all-reduce.2.cloned.1.call-start = ((), (), s32[]{:S(2)}) async-start(), calls=%async_computation.4 | async-start | bytes 2064384 | tf_op jit(solution)/shard_map/psum | solution.py:76
  206.4 0.8 copy-start.3
  206.4 13.6 %collective-permute-start = (bf16[1,512,500]{1,2,0:T(8,128)(2,1)S(1)}, bf16[1,512,500]{1,2,0:T(8,128)(2,1)}, u32[]{:S(2)}, u32[]{:S(2)}) collective-permute-start(bf16[1,512,500]{1,2,0:T(8,128)(2,1)S(1)} %get-tuple-element.6), channel_id=1, source_target_pairs={{0,4},{4,0},{8,12},{12,8},{1,5},{5,1},{9,13},{13,9},{2,6},{6,2},{1... | collective-permute-start | bytes 1536008 | tf_op jit(solution)/shard_map/ppermute | solution.py:23
  223.2 46.7 %collective-permute-start.1 = (bf16[2,512,500]{1,0,2:T(2,128)(2,1)}, bf16[2,512,500]{1,0,2:T(2,128)(2,1)}, u32[]{:S(2)}, u32[]{:S(2)}) collective-permute-start(bf16[2,512,500]{1,0,2:T(2,128)(2,1)} %copy.10), channel_id=1, source_target_pairs={{0,8},{4,12},{8,0},{12,4},{1,9},{5,13},{9,1},{13,5},{2,10},{6,14},... | collective-permute-start | bytes 3072008 | tf_op jit(solution)/shard_map/ppermute | solution.py:23
  277.0 43.3 %copy-start.2 = (f32[512,500]{0,1:T(8,128)S(1)}, f32[512,500]{0,1:T(8,128)}, u32[]{:S(2)}) copy-start(f32[512,500]{0,1:T(8,128)} %param.12) | copy-start | bytes 3072004
Sparse Core Ops, SparseCore 0:
  18.8 13.2 all-gather.2
  37.0 76.9 reduce-scatter.1
  115.7 80.1 all-gather.4
  281.6 38.5 all-reduce.1
